TPU v7x, 32 devices: a whole 2x2x4 slice. The times are simulated.
32 devices in a mesh: prow: 8 (over y, x, core), pcol: 4 (over z).
Axes of the slice: x: 2, y: 2, z: 4, core: 2. Of those that a mesh axis runs over, the one named last changes fastest.
Arguments:
- inverse_trailing: bfloat16 [18432, 18432], P('prow', 'pcol'), may hold values from -6 to 6
- panel: bfloat16 [18432, 256], P('prow'), may hold values from -0.0625 to 0.0625
- supernode_inverse: float32 [256, 256], replicated, may hold values from -6 to 6
- block_live: int32 [72], replicated, may hold values from 0 to 1, as said below
Outputs:
- column_inverse: float32 [18432, 256], P('prow')
- diagonal_inverse: float32 [256, 256], replicated
Inputs may be any that keep to these rules, and one draw needn't show every extreme that they name: Each aligned group of 9 consecutive block rows (the rows of one index of prow) holds at least one block row with block_live 1.
All inputs are finite; a program needn't handle non-finite values.
Results may differ from a plain program's by a relative error of at most 0.0003.
Values may be sent and summed in bfloat16 or wider, within the bound.
No kernel may reach another device: no remote copies, remote signals or barrier semaphores. Data moves between devices by JAX's collectives and lax.ppermute only.
A program may use at most 128 MiB of HBM per device.

v0:
```python
import jax
import jax.numpy as jnp
from jax import lax
from jax.sharding import PartitionSpec as P


def from_root(block, axis, source):
    block = jnp.where(lax.axis_index(axis) == source, block, jnp.zeros_like(block))
    return lax.psum(block, axis)


def per_device(inverse_trailing, panel, supernode_inverse, block_live):
    rows_dev = panel.shape[0]
    width = panel.shape[1]
    col_count = inverse_trailing.shape[1]
    ratio = lax.axis_size("prow") // lax.axis_size("pcol")
    row_index = lax.axis_index("prow")
    col_index = lax.axis_index("pcol")
    live_all = jnp.repeat(block_live, width)
    col_live = lax.dynamic_slice_in_dim(live_all, col_index * col_count, col_count).astype(
        jnp.float32
    )
    row_live = lax.dynamic_slice_in_dim(live_all, row_index * rows_dev, rows_dev).astype(
        jnp.float32
    )
    partial_sum = jnp.zeros((rows_dev, width), jnp.float32)
    for half in range(ratio):
        received = from_root(panel, "prow", col_index * ratio + half)
        half_live = col_live[half * rows_dev : (half + 1) * rows_dev]
        masked_half = (received.astype(jnp.float32) * half_live[:, None]).astype(jnp.bfloat16)
        tile_cols = inverse_trailing[:, half * rows_dev : (half + 1) * rows_dev]
        partial_sum = partial_sum + jnp.dot(
            tile_cols, masked_half, preferred_element_type=jnp.float32
        )
    local_panel = panel.astype(jnp.float32) * row_live[:, None]
    contract_rows = (((0,), (0,)), ((), ()))
    total = lax.psum(partial_sum, "pcol")
    column_inverse = -total * row_live[:, None]
    term = lax.dot_general(
        local_panel, column_inverse, contract_rows, precision=lax.Precision.HIGHEST
    )
    diag_total = lax.psum(term, "prow")
    diagonal_inverse = supernode_inverse - diag_total
    return (column_inverse, diagonal_inverse)


def solution(mesh):
    in_specs = (P("prow", "pcol"), P("prow", None), P(), P())
    out_specs = (P("prow", None), P())
    return jax.shard_map(
        per_device, mesh=mesh, in_specs=in_specs, out_specs=out_specs, check_vma=False
    )
```

profile of v0, /device:TPU:0, one launch (start us, length us, event | category | flops | bytes accessed | tf_op | source)
XLA Modules:
  0.0 254.0 jit_solution(5009432006979550034)
XLA Ops:
  7.2 0.0 copy-start
  7.2 0.0 all-reduce.9.cloned.1.call-start
  7.2 2.8 %broadcast_select_fusion.1 = (bf16[2304,256]{1,0:T(8,128)(2,1)}, bf16[2304,256]{1,0:T(8,128)(2,1)}) fusion(bf16[2304,256]{1,0:T(8,128)(2,1)} %param.5, pred[]{:T(512)S(6)} %eq.6, pred[]{:T(512)S(6)} %eq.7), kind=kLoop, calls=%fused_computation.16 | loop fusion | flops 1179648 | bytes 3538946 | tf_op jit(solution)/shard_map/jit(_where)/select_n | solution.py:8
  10.1 0.0 all-reduce.9.cloned.1.call-update
  10.1 0.0 all-reduce.5.cloned.1.call-start
  10.2 0.0 copy-done
  10.2 0.1 broadcast_bitcast_fusion
  10.3 0.1 dynamic-slice_convert_fusion
  10.4 67.3 %all-reduce.9.cloned.1.call-done = (bf16[2304,256]{1,0:T(8,128)(2,1)}, bf16[2304,256]{1,0:T(8,128)(2,1)}) async-done(((bf16[2304,256]{1,0:T(8,128)(2,1)}, bf16[2304,256]{1,0:T(8,128)(2,1)}), (bf16[2304,256]{1,0:T(8,128)(2,1)}, bf16[2304,256]{1,0:T(8,128)(2,1)})) %all-reduce.9.cloned.1.call-update) | async-done | bytes 2359312 | tf_op jit(solution)/shard_map/psum | solution.py:9
  77.6 0.0 copy-start.3
  77.7 7.3 %fusion = f32[256,2304]{1,0:T(8,128)S(1)} fusion(bf16[2304,4608]{1,0:T(8,128)(2,1)} %param.4, bf16[2304,256]{1,0:T(8,128)(2,1)} %get-tuple-element.4, f32[2304]{0:T(1024)S(1)} %get-tuple-element.9), kind=kOutput, calls=%fused_computation | convolution fusion | flops 2719678464 | bytes 14164992 | tf_op jit(solution)/shard_map/dot_general | solution.py:32
  85.0 0.0 copy-done.3
  85.0 8.9 %fusion.7 = f32[2304,256]{0,1:T(8,128)} fusion(f32[256,2304]{1,0:T(8,128)S(1)} %fusion, bf16[2304,4608]{1,0:T(8,128)(2,1)} %param.4, bf16[2304,256]{1,0:T(8,128)(2,1)S(1)} %copy-done.3, f32[2304]{0:T(1024)S(1)} %get-tuple-element.8), kind=kOutput, calls=%fused_computation.5 | convolution fusion | flops 2720268288 | bytes 16524288 | tf_op jit(solution)/shard_map/dot_general | solution.py:32
  93.9 0.0 copy-start.1
  93.9 0.0 all-reduce.5.cloned.1.call-update
  93.9 0.0 all-reduce.7.cloned.1.call-start
  94.0 1.2 copy-done.1
  95.2 0.7 copy.6
  95.9 0.1 dynamic-slice_convert_fusion.1
  96.0 92.0 %all-reduce.5.cloned.1.call-done = f32[2304,256]{0,1:T(8,128)} async-done(((f32[2304,256]{0,1:T(8,128)}), f32[2304,256]{0,1:T(8,128)}) %all-reduce.5.cloned.1.call-update) | async-done | bytes 2359312 | tf_op jit(solution)/shard_map/psum | solution.py:37
  188.0 4.7 %fusion.10 = f32[256,256]{1,0:T(8,128)} fusion(bf16[2304,256]{0,1:T(8,128)(2,1)S(1)} %copy.6, f32[2304]{0:T(1024)S(1)} %dynamic-slice_convert_fusion.1, f32[2304,256]{0,1:T(8,128)} %all-reduce.5.cloned.1.call-done), kind=kOutput, calls=%fused_computation.6 | convolution fusion | flops 1814298624 | bytes 3810304 | tf_op jit(solution)/shard_map/dot_general | solution.py:39
  192.7 0.0 all-reduce.7.cloned.1.call-update
  192.7 1.8 negate_multiply_fusion
  194.6 0.0 copy-start.2
  194.6 2.0 copy.7
  196.5 49.3 %all-reduce.7.cloned.1.call-done = f32[256,256]{1,0:T(8,128)} async-done(((f32[256,256]{1,0:T(8,128)}), f32[256,256]{1,0:T(8,128)}) %all-reduce.7.cloned.1.call-update) | async-done | bytes 262160 | tf_op jit(solution)/shard_map/psum | solution.py:42
  245.8 0.0 copy-done.2
  245.8 1.7 sub.3
  (2 shorter events, 0.0 us)
Async XLA Ops:
  7.2 3.0 %copy-start = (s32[72]{0:T(128)S(1)}, s32[72]{0:T(128)}, u32[]{:S(2)}) copy-start(s32[72]{0:T(128)} %param.7) | copy-start | bytes 868
  7.2 70.5 %all-reduce.9.cloned.1.call-start = ((), (), s32[]{:S(2)}) async-start(), calls=%async_computation.2 | async-start | bytes 4718592 | tf_op jit(solution)/shard_map/psum | solution.py:9
  10.1 177.9 %all-reduce.5.cloned.1.call-start = ((), (), s32[]{:S(2)}) async-start(), calls=%async_computation | async-start | bytes 4718592 | tf_op jit(solution)/shard_map/psum | solution.py:37
  77.6 7.3 %copy-start.3 = (bf16[2304,256]{1,0:T(8,128)(2,1)S(1)}, bf16[2304,256]{1,0:T(8,128)(2,1)}, u32[]{:S(2)}) copy-start(bf16[2304,256]{1,0:T(8,128)(2,1)} %get-tuple-element.5) | copy-start | bytes 3538948
  93.9 1.3 copy-start.1
  93.9 151.9 %all-reduce.7.cloned.1.call-start = ((), (), s32[]{:S(2)}) async-start(), calls=%async_computation.1 | async-start | bytes 524288 | tf_op jit(solution)/shard_map/psum | solution.py:42
  194.6 51.2 %copy-start.2 = (f32[256,256]{1,0:T(8,128)S(1)}, f32[256,256]{1,0:T(8,128)}, u32[]{:S(2)}) copy-start(f32[256,256]{1,0:T(8,128)} %param.6) | copy-start | bytes 786436
Sparse Core Ops, SparseCore 0:
  11.9 65.7 all-reduce.8
  94.0 93.9 all-reduce.4
  192.9 52.9 all-reduce.6
where the time goes:
time: 254 us
  waiting for transfers between devices  209 us (82%)
  matrix products  20.9 us (8%)
  between operations  13.8 us (5%)
  other arithmetic  6.55 us (3%)
  local copies, waits for them, and re-layouts  4.01 us (2%)
    psum x1, waiting for transfers between devices, per_device(): total = lax.psum(partial_sum, 'pcol')  92 us
    psum x1, waiting for transfers between devices, from_root(): return lax.psum(block, axis)  67.3 us
    psum x1, waiting for transfers between devices, per_device(): diag_total = lax.psum(term, 'prow')  49.3 us
    dot_general x2, matrix products, per_device(): jnp.dot(tile_cols, masked_half, preferred_element_type=jnp.float32)  16.2 us
  transfers between devices with their start and end apart: 3, of which 3 were waited for; matrix products, arithmetic and copies ran while one was open for 2% of the time, Pallas kernels for 0%

commit v1 on v0

--- a/solution.py
+++ b/solution.py
@@ -2,6 +2,11 @@
 import jax.numpy as jnp
 from jax import lax
 from jax.sharding import PartitionSpec as P
+from jax.lax import all_gather
+
+
+def _convert_meshes(frame):
+    return jnp.sum(all_gather(frame, "prow"), axis=0)
 
 
 def from_root(block, axis, source):
@@ -39,7 +44,7 @@
     term = lax.dot_general(
         local_panel, column_inverse, contract_rows, precision=lax.Precision.HIGHEST
     )
-    diag_total = lax.psum(term, "prow")
+    diag_total = _convert_meshes(term)
     diagonal_inverse = supernode_inverse - diag_total
     return (column_inverse, diagonal_inverse)
 

time: 254 us -> 229 us (0.902)
  waiting for transfers between devices: 209 us -> 183 us
    psum x1 -> x0, waiting for transfers between devices: 49.3 us -> none  [per_device(): diag_total = lax.psum(term, 'prow')]
    all_gather x0 -> x1, waiting for transfers between devices: none -> 23.2 us  [_convert_meshes(): return jnp.sum(all_gather(frame, 'prow'), axis=0)]
where the time goes in v1:
time: 229 us
  waiting for transfers between devices  183 us (80%)
  matrix products  20.9 us (9%)
  between operations  13.8 us (6%)
  other arithmetic  7.34 us (3%)
  local copies, waits for them, and re-layouts  4 us (2%)
    psum x1, waiting for transfers between devices, per_device(): total = lax.psum(partial_sum, 'pcol')  92 us
    psum x1, waiting for transfers between devices, from_root(): return lax.psum(block, axis)  67.3 us
    all_gather x1, waiting for transfers between devices, _convert_meshes(): return jnp.sum(all_gather(frame, 'prow'), axis=0)  23.2 us
    dot_general x2, matrix products, per_device(): jnp.dot(tile_cols, masked_half, preferred_element_type=jnp.float32)  16.2 us
    dot_general x1, matrix products, per_device(): lax.dot_general(local_panel, column_inverse, contract_rows, precision=lax...  4.7 us
  transfers between devices with their start and end apart: 3, of which 3 were waited for; matrix products, arithmetic and copies ran while one was open for 2% of the time, Pallas kernels for 0%

profile of v1, /device:TPU:0, one launch (start us, length us, event | category | flops | bytes accessed | tf_op | source)
XLA Modules:
  0.0 228.7 jit_solution(10002361908651925015)
XLA Ops:
  7.2 0.0 copy-start
  7.2 0.0 all-reduce.6.cloned.1.call-start
  7.2 2.8 %broadcast_select_fusion.1 = (bf16[2304,256]{1,0:T(8,128)(2,1)}, bf16[2304,256]{1,0:T(8,128)(2,1)}) fusion(bf16[2304,256]{1,0:T(8,128)(2,1)} %param.5, pred[]{:T(512)S(6)} %eq.6, pred[]{:T(512)S(6)} %eq.7), kind=kLoop, calls=%fused_computation.16 | loop fusion | flops 1179648 | bytes 3538946 | tf_op jit(solution)/shard_map/jit(_where)/select_n | solution.py:13
  10.1 0.0 all-reduce.6.cloned.1.call-update
  10.1 0.0 all-reduce.4.cloned.1.call-start
  10.2 0.0 copy-done
  10.2 0.1 broadcast_bitcast_fusion
  10.3 0.1 dynamic-slice_convert_fusion
  10.4 67.3 %all-reduce.6.cloned.1.call-done = (bf16[2304,256]{1,0:T(8,128)(2,1)}, bf16[2304,256]{1,0:T(8,128)(2,1)}) async-done(((bf16[2304,256]{1,0:T(8,128)(2,1)}, bf16[2304,256]{1,0:T(8,128)(2,1)}), (bf16[2304,256]{1,0:T(8,128)(2,1)}, bf16[2304,256]{1,0:T(8,128)(2,1)})) %all-reduce.6.cloned.1.call-update) | async-done | bytes 2359312 | tf_op jit(solution)/shard_map/psum | solution.py:14
  77.6 0.0 copy-start.3
  77.7 7.3 %fusion = f32[256,2304]{1,0:T(8,128)S(1)} fusion(bf16[2304,4608]{1,0:T(8,128)(2,1)} %param.4, bf16[2304,256]{1,0:T(8,128)(2,1)} %get-tuple-element.4, f32[2304]{0:T(1024)S(1)} %get-tuple-element.9), kind=kOutput, calls=%fused_computation | convolution fusion | flops 2719678464 | bytes 14164992 | tf_op jit(solution)/shard_map/dot_general | solution.py:37
  85.0 0.0 copy-done.3
  85.0 8.9 %fusion.7 = f32[2304,256]{0,1:T(8,128)} fusion(f32[256,2304]{1,0:T(8,128)S(1)} %fusion, bf16[2304,4608]{1,0:T(8,128)(2,1)} %param.4, bf16[2304,256]{1,0:T(8,128)(2,1)S(1)} %copy-done.3, f32[2304]{0:T(1024)S(1)} %get-tuple-element.8), kind=kOutput, calls=%fused_computation.5 | convolution fusion | flops 2720268288 | bytes 16524288 | tf_op jit(solution)/shard_map/dot_general | solution.py:37
  93.9 0.0 copy-start.1
  93.9 0.0 all-reduce.4.cloned.1.call-update
  93.9 0.0 all-gather.3.cloned.1.call-start
  94.0 1.2 copy-done.1
  95.2 0.7 copy.6
  95.9 0.1 dynamic-slice_convert_fusion.1
  96.0 92.0 %all-reduce.4.cloned.1.call-done = f32[2304,256]{0,1:T(8,128)} async-done(((f32[2304,256]{0,1:T(8,128)}), f32[2304,256]{0,1:T(8,128)}) %all-reduce.4.cloned.1.call-update) | async-done | bytes 2359312 | tf_op jit(solution)/shard_map/psum | solution.py:42
  188.0 4.7 %fusion.10 = f32[256,256]{1,0:T(8,128)} fusion(bf16[2304,256]{0,1:T(8,128)(2,1)S(1)} %copy.6, f32[2304]{0:T(1024)S(1)} %dynamic-slice_convert_fusion.1, f32[2304,256]{0,1:T(8,128)} %all-reduce.4.cloned.1.call-done), kind=kOutput, calls=%fused_computation.6 | convolution fusion | flops 1814298624 | bytes 3810304 | tf_op jit(solution)/shard_map/dot_general | solution.py:44
  192.7 0.0 all-gather.3.cloned.1.call-update
  192.7 1.8 negate_multiply_fusion
  194.6 2.0 copy.7
  196.5 0.0 copy-start.2
  196.5 23.2 %all-gather.3.cloned.1.call-done = f32[2048,256]{1,0:T(8,128)} async-done(((f32[256,256]{1,0:T(8,128)}), f32[2048,256]{1,0:T(8,128)}) %all-gather.3.cloned.1.call-update) | async-done | bytes 2097168 | tf_op jit(solution)/shard_map/all_gather | solution.py:9
  219.7 1.8 reduce_sum.9
  221.5 0.0 copy-done.2
  221.5 0.7 sub.3
  (2 shorter events, 0.0 us)
Async XLA Ops:
  7.2 3.0 %copy-start = (s32[72]{0:T(128)S(1)}, s32[72]{0:T(128)}, u32[]{:S(2)}) copy-start(s32[72]{0:T(128)} %param.7) | copy-start | bytes 868
  7.2 70.5 %all-reduce.6.cloned.1.call-start = ((), (), s32[]{:S(2)}) async-start(), calls=%async_computation.2 | async-start | bytes 4718592 | tf_op jit(solution)/shard_map/psum | solution.py:14
  10.1 177.9 %all-reduce.4.cloned.1.call-start = ((), (), s32[]{:S(2)}) async-start(), calls=%async_computation | async-start | bytes 4718592 | tf_op jit(solution)/shard_map/psum | solution.py:42
  77.6 7.3 %copy-start.3 = (bf16[2304,256]{1,0:T(8,128)(2,1)S(1)}, bf16[2304,256]{1,0:T(8,128)(2,1)}, u32[]{:S(2)}) copy-start(bf16[2304,256]{1,0:T(8,128)(2,1)} %get-tuple-element.5) | copy-start | bytes 3538948
  93.9 1.3 copy-start.1
  93.9 125.8 %all-gather.3.cloned.1.call-start = ((), (), s32[]{:S(2)}) async-start(), calls=%async_computation.1 | async-start | bytes 2359296 | tf_op jit(solution)/shard_map/all_gather | solution.py:9
  196.5 24.9 %copy-start.2 = (f32[256,256]{1,0:T(8,128)S(1)}, f32[256,256]{1,0:T(8,128)}, u32[]{:S(2)}) copy-start(f32[256,256]{1,0:T(8,128)} %param.6) | copy-start | bytes 786436
Sparse Core Ops, SparseCore 0:
  11.9 65.7 all-reduce.5
  94.0 93.9 all-reduce.3
  192.9 26.7 all-gather.2
